TPU v7x, 32 devices: a whole 2x2x4 slice. The times are simulated.
32 devices in a mesh: groups: 2 (over y), chol: 4 (over z), walk: 2 (over x), orb: 2 (over core).
Axes of the slice: x: 2, y: 2, z: 4, core: 2. Of those that a mesh axis runs over, the one named last changes fastest.
Arguments:
- walkers: float32 [32, 2, 36864], P(('groups', 'walk'), None, ('chol', 'orb')), parts along dimension 0, may hold values from -6 to 6
- correlation_inverse: float32 [32, 2, 96, 96], P(('groups', 'walk')), parts along dimension 0, may hold values from -0.625 to 0.625
- half_vectors: bfloat16 [4096, 36864], P(('groups', 'walk'), ('chol', 'orb')), parts along dimension 0, may hold values from -0.01953125 to 0.01953125
- field_vectors: bfloat16 [4096, 384, 384], P(('groups', 'walk'), ('chol', 'orb')), parts along dimension 0, may hold values from -0.0048828125 to 0.0048828125
- samples: float32 [32, 2048], P('groups', 'walk'), parts along dimension 0, may hold values from -6 to 6
- source: int32 [32], P(('groups', 'walk')), parts along dimension 0, may hold values from 0 to 15
Outputs:
- walkers_next: float32 [32, 2, 36864], P(('groups', 'walk'), None, ('chol', 'orb')), parts along dimension 0
There are 2 independent parts, one for each index of `groups`. A program takes and returns all parts, laid end to end along the dimension named above; each array names one. Nothing has to cross between parts.
All inputs are finite; a program needn't handle non-finite values.
Results may differ from a plain program's by a relative error of at most 0.02.
Values may be sent and summed in bfloat16 or wider, within the bound.
No kernel may reach another device: no remote copies, remote signals or barrier semaphores. Data moves between devices by JAX's collectives and lax.ppermute only.
A program may use at most 128 MiB of HBM per device.

v0:
```python
import jax
import jax.numpy as jnp
from jax import lax
from jax.sharding import PartitionSpec as P

TERMS = 4
NS_STEPS = 2


def for_sending(shard):
    return jax.tree.map(lambda a: a.astype(jnp.bfloat16) if a.dtype == jnp.float32 else a, shard)


def complex_product(left_real, left_imag, right_real, right_imag, formula):
    first = jnp.einsum(formula, left_real, right_real, precision=lax.Precision.HIGHEST)
    second = jnp.einsum(formula, left_imag, right_imag, precision=lax.Precision.HIGHEST)
    third = jnp.einsum(formula, left_real, right_imag, precision=lax.Precision.HIGHEST)
    fourth = jnp.einsum(formula, left_imag, right_real, precision=lax.Precision.HIGHEST)
    return (first - second, third + fourth)


def normalizer(gram_real, gram_imag):
    electrons = gram_real.shape[-1]
    identity = jnp.eye(electrons, dtype=jnp.float32)
    scale_factor = jnp.trace(gram_real, axis1=1, axis2=2) / electrons
    iter_real = gram_real / scale_factor[:, None, None]
    iter_imag = gram_imag / scale_factor[:, None, None]
    root_real = jnp.broadcast_to(identity, gram_real.shape)
    root_imag = jnp.zeros_like(gram_real)
    for sweep_index in range(NS_STEPS):
        prod_real, prod_imag = complex_product(
            root_real, root_imag, iter_real, iter_imag, "wij,wjk->wik"
        )
        step_real = 1.5 * identity - 0.5 * prod_real
        step_imag = -0.5 * prod_imag
        iter_real, iter_imag = complex_product(
            iter_real, iter_imag, step_real, step_imag, "wij,wjk->wik"
        )
        root_real, root_imag = complex_product(
            step_real, step_imag, root_real, root_imag, "wij,wjk->wik"
        )
    inverse_root = lax.rsqrt(scale_factor)[:, None, None]
    return (root_real * inverse_root, root_imag * inverse_root)


def field_apply(field_block, values):
    next_real = jnp.einsum(
        "wab,wbn->wan", field_block[:, 0], values[:, 0], preferred_element_type=jnp.float32
    )
    next_real = next_real - jnp.einsum(
        "wab,wbn->wan", field_block[:, 1], values[:, 1], preferred_element_type=jnp.float32
    )
    next_imag = jnp.einsum(
        "wab,wbn->wan", field_block[:, 0], values[:, 1], preferred_element_type=jnp.float32
    )
    next_imag = next_imag + jnp.einsum(
        "wab,wbn->wan", field_block[:, 1], values[:, 0], preferred_element_type=jnp.float32
    )
    return jnp.stack([next_real, next_imag], 1)


def body(walkers, correlation_inverse, half_vectors, field_vectors, samples, source):
    local_walkers = walkers.shape[0]
    row_block = field_vectors.shape[1]
    orbitals = field_vectors.shape[2]
    electrons = correlation_inverse.shape[2]
    grid = walkers.reshape(local_walkers, 2, row_block, electrons)
    theta_real, theta_imag = complex_product(
        grid[:, 0], grid[:, 1], correlation_inverse[:, 0], correlation_inverse[:, 1], "wmk,wkn->wmn"
    )
    theta = (
        jnp.stack([theta_real, theta_imag], 1)
        .reshape(local_walkers, 2, row_block * electrons)
        .astype(jnp.bfloat16)
    )
    all_theta = lax.all_gather(theta, "walk", axis=0, tiled=True)
    bias_part = jnp.einsum(
        "wcj,gj->wcg", all_theta, half_vectors, preferred_element_type=jnp.float32
    )
    bias = lax.psum(bias_part, ("chol", "orb"))
    coefficient = jnp.stack([bias[:, 1], samples - bias[:, 0]], 1).astype(jnp.bfloat16)
    field_part = jnp.einsum(
        "wcg,gab->wcab", coefficient, field_vectors, preferred_element_type=jnp.float32
    )
    field = lax.psum_scatter(field_part, "walk", scatter_dimension=0, tiled=True).astype(
        jnp.bfloat16
    )
    devices_rows = lax.axis_size(("chol", "orb"))
    sharers = devices_rows // local_walkers
    col_width = electrons // sharers
    parted = grid.reshape(local_walkers, 2, row_block, sharers, col_width)
    parted = parted.transpose(0, 3, 1, 2, 4).reshape(devices_rows, 2, row_block, col_width)
    columns = lax.all_to_all(
        parted.astype(jnp.bfloat16), ("chol", "orb"), split_axis=0, concat_axis=2, tiled=True
    ).astype(parted.dtype)
    spread = jnp.broadcast_to(field[:, None], (local_walkers, sharers, 2, row_block, orbitals))
    spread = spread.reshape(devices_rows, 2, row_block, orbitals)
    whole_field = lax.all_to_all(spread, ("chol", "orb"), split_axis=0, concat_axis=2, tiled=True)
    current = columns
    col_summed = columns
    for order_index in range(1, TERMS + 1):
        current = field_apply(whole_field, current.astype(jnp.bfloat16)) / order_index
        col_summed = col_summed + current
    returned = lax.all_to_all(
        col_summed.astype(jnp.bfloat16), ("chol", "orb"), split_axis=2, concat_axis=0, tiled=True
    ).astype(col_summed.dtype)
    returned = returned.reshape(local_walkers, sharers, 2, row_block, col_width)
    summed = returned.transpose(0, 2, 3, 1, 4).reshape(local_walkers, 2, row_block, electrons)
    whole = lax.all_gather(summed.astype(jnp.bfloat16), ("chol", "orb"), axis=2, tiled=True).astype(
        summed.dtype
    )
    gram_real, gram_imag = complex_product(
        whole[:, 0], -whole[:, 1], whole[:, 0], whole[:, 1], "wmi,wmj->wij"
    )
    gram_real = gram_real / orbitals
    gram_imag = gram_imag / orbitals
    root_real, root_imag = normalizer(gram_real, gram_imag)
    norm_real, norm_imag = complex_product(
        summed[:, 0], summed[:, 1], root_real, root_imag, "wmk,wkn->wmn"
    )
    normalized = jnp.stack([norm_real, norm_imag], 1).reshape(
        local_walkers, 2, row_block * electrons
    )
    moved = lax.all_gather(for_sending(normalized), "walk", axis=0, tiled=True).astype(
        normalized.dtype
    )
    return jnp.take(moved, source, axis=0)


def solution(mesh):
    placed = (
        P(("groups", "walk"), None, ("chol", "orb")),
        P(("groups", "walk"), None, None, None),
        P(("groups", "walk"), ("chol", "orb")),
        P(("groups", "walk"), ("chol", "orb"), None),
        P("groups", "walk"),
        P(("groups", "walk")),
    )
    return jax.shard_map(
        body,
        mesh=mesh,
        in_specs=placed,
        out_specs=P(("groups", "walk"), None, ("chol", "orb")),
        check_vma=False,
    )
```

profile of v0, /device:TPU:0, one launch (start us, length us, event | category | flops | bytes accessed | tf_op | source)
XLA Modules:
  0.0 241.8 jit_solution(14504771620466679729)
XLA Ops:
  6.5 1.1 copy.45
  7.8 0.5 fusion.37
  8.3 0.5 fusion.41
  8.7 0.5 fusion.29
  9.4 0.5 fusion.28
  10.0 7.5 %all_gather.9 = bf16[16,2,4608]{2,0,1:T(8,128)(2,1)S(1)} all-gather(bf16[8,2,4608]{2,0,1:T(8,128)(2,1)S(1)} %pad_maximum_fusion.1), channel_id=1, replica_groups=mesh['groups'=2,'chol'=4,'walk'=2,'orb'=2] {'walk'}, dimensions={0}, use_global_device_ids=true | all-gather | bytes 442368 | tf_op jit(solution)/shard_map/all_gather | solution.py:76
  17.5 7.2 %fusion.3 = f32[16,2,1024]{2,0,1:T(8,128)} fusion(bf16[16,2,4608]{2,0,1:T(8,128)(2,1)S(1)} %all_gather.9, bf16[1024,4608]{1,0:T(8,128)(2,1)} %param.8), kind=kOutput, calls=%fused_computation.4 | convolution fusion | flops 301989888 | bytes 9863168 | tf_op jit(solution)/shard_map/wcj,gj->wcg/dot_general | solution.py:77
  25.0 56.4 %all-reduce.2.cloned.1.call-done = f32[16,2,1024]{2,0,1:T(8,128)} async-done(((f32[16,2,1024]{2,0,1:T(8,128)}), f32[16,2,1024]{2,0,1:T(8,128)}) %all-reduce.2.cloned.1.call-update) | async-done | bytes 131088 | tf_op jit(solution)/shard_map/psum | solution.py:80
  81.4 0.8 slice.232
  82.2 0.8 fusion.78
  83.1 29.4 %fusion = f32[16,2,48,384]{3,0,2,1:T(8,128)} fusion(bf16[1024,48,384]{2,1,0:T(8,128)(2,1)} %param.9, bf16[16,1,1024]{2,0,1:T(8,128)(2,1)S(1)} %fusion.78, bf16[16,1,1024]{2,0,1:T(8,128)(2,1)S(1)} %slice.232), kind=kOutput, calls=%fused_computation.1 | convolution fusion | flops 1208090624 | bytes 40173568 | tf_op jit(solution)/shard_map/wcg,gab->wcab/dot_general | solution.py:82
  112.5 0.7 copy.46
  113.2 3.4 %all-to-all-start = ((bf16[8,2,48,96]{3,2,1,0:T(8,128)(2,1)}), bf16[8,2,48,96]{3,2,1,0:T(8,128)(2,1)S(1)}, u32[]{:S(2)}, u32[]{:S(2)}) async-start(bf16[8,2,48,96]{3,2,1,0:T(8,128)(2,1)} %copy.46), calls=%async_computation | async-start | bytes 393216 | tf_op jit(solution)/shard_map/all_to_all | solution.py:93
  116.6 29.9 %reduce-scatter.2.cloned.1.call-done = f32[8,2,48,384]{3,0,2,1:T(8,128)} async-done(((f32[16,2,48,384]{3,0,2,1:T(8,128)}), f32[8,2,48,384]{3,0,2,1:T(8,128)}) %reduce-scatter.2.cloned.1.call-update) | async-done | bytes 1179664 | tf_op jit(solution)/shard_map/reduce_scatter | solution.py:85
  146.5 1.3 convert_element_type.82
  147.8 0.9 copy.52
  148.7 4.6 %all-to-all-start.1 = ((bf16[8,2,48,384]{3,2,1,0:T(8,128)(2,1)}), bf16[8,2,48,384]{3,2,1,0:T(8,128)(2,1)S(1)}, u32[]{:S(2)}, u32[]{:S(2)}) async-start(bf16[8,2,48,384]{3,2,1,0:T(8,128)(2,1)} %copy.52), calls=%async_computation.2 | async-start | bytes 1179648 | tf_op jit(solution)/shard_map/all_to_all | solution.py:98
  153.3 0.3 all-gather.3.cloned.1.call-start
  153.8 16.3 %all-to-all-done.1 = bf16[8,2,48,384]{3,2,1,0:T(8,128)(2,1)S(1)} async-done(((bf16[8,2,48,384]{3,2,1,0:T(8,128)(2,1)}), bf16[8,2,48,384]{3,2,1,0:T(8,128)(2,1)S(1)}, u32[]{:S(2)}, u32[]{:S(2)}) %all-to-all-start.1) | async-done | bytes 589856 | tf_op jit(solution)/shard_map/all_to_all | solution.py:98
  170.1 0.3 fusion.65
  170.4 0.3 fusion.64
  170.7 0.3 fusion.26
  170.9 0.3 fusion.27
  171.7 0.2 fusion.24
  172.0 0.2 fusion.25
  172.5 0.2 fusion.74
  172.7 0.2 fusion.22
  172.9 0.2 fusion.23
  174.4 10.7 %all_to_all.54 = bf16[1,2,384,96]{3,1,0,2:T(2,128)(2,1)S(1)} all-to-all(bf16[1,2,384,96]{3,1,0,2:T(2,128)(2,1)S(1)} %copy.54), channel_id=1, replica_groups=mesh['groups'=2,'chol'=4,'walk'=2,'orb'=2] {'chol','orb'}, dimensions={2} | all-to-all | bytes 294912 | tf_op jit(solution)/shard_map/all_to_all | solution.py:104
  185.2 0.7 copy.56
  186.0 23.3 %all-gather.3.cloned.1.call-done = bf16[8,1,2,384,96]{4,0,2,1,3:T(8,128)(2,1)} async-done(((bf16[8,1,2,48,96]{4,0,2,1,3:T(8,128)(2,1)}), bf16[8,1,2,384,96]{4,0,2,1,3:T(8,128)(2,1)}) %all-gather.3.cloned.1.call-update) | async-done | bytes 1179664 | tf_op jit(solution)/shard_map/all_gather | solution.py:109
  209.3 2.1 copy.57
  211.4 0.8 fusion.18
  212.2 0.8 fusion.16
  213.1 0.4 select_reduce_fusion
  213.5 0.4 fusion.7
  213.9 0.5 fusion.62
  214.5 0.5 fusion.58
  214.9 0.5 fusion.15
  215.4 0.5 fusion.60
  215.9 0.6 fusion.88
  216.5 0.5 fusion.52
  217.0 0.5 fusion.13
  217.5 0.6 fusion.87
  218.1 0.5 convolution_subtract_fusion.4
  218.6 0.5 convolution_subtract_fusion.3
  219.1 0.5 convolution_add_fusion.4
  219.6 0.5 convolution_add_fusion.3
  220.2 0.5 fusion.89
  220.7 0.5 fusion.91
  221.2 0.5 fusion.12
  221.8 0.5 fusion.92
  222.3 0.5 fusion.90
  222.9 0.5 fusion.10
  223.4 0.5 fusion.8
  223.9 0.8 fusion.9
  224.8 0.3 fusion.66
  225.1 0.3 fusion.67
  225.4 0.3 fusion.31
  225.9 0.3 fusion.30
  226.3 0.3 pad_maximum_fusion.2
  226.7 6.6 %all_gather.11 = bf16[16,2,4608]{2,1,0:T(2,128)(2,1)S(1)} all-gather(bf16[8,2,4608]{2,1,0:T(2,128)(2,1)S(1)} %pad_maximum_fusion.2), channel_id=1, replica_groups=mesh['groups'=2,'chol'=4,'walk'=2,'orb'=2] {'walk'}, dimensions={0}, use_global_device_ids=true | all-gather | bytes 442368 | tf_op jit(solution)/shard_map/all_gather | solution.py:124
  233.5 0.9 gather_fusion
  234.4 0.9 broadcast_select_fusion
  (43 shorter events, 3.6 us)
Async XLA Ops:
  6.5 1.3 copy-start
  6.5 74.9 %all-reduce.2.cloned.1.call-start = ((), (), s32[]{:S(2)}) async-start(), calls=%async_computation.4 | async-start | bytes 262144 | tf_op jit(solution)/shard_map/psum | solution.py:80
  17.5 64.7 %copy-start.1 = (f32[16,1024]{1,0:T(8,128)S(1)}, f32[16,1024]{1,0:T(8,128)}, u32[]{:S(2)}) copy-start(f32[16,1024]{1,0:T(8,128)} %param.10) | copy-start | bytes 196612
  24.7 121.7 %reduce-scatter.2.cloned.1.call-start = ((), (), s32[]{:S(2)}) async-start(), calls=%async_computation.5 | async-start | bytes 3538944 | tf_op jit(solution)/shard_map/reduce_scatter | solution.py:85
  113.2 35.5 %all-to-all-start = ((bf16[8,2,48,96]{3,2,1,0:T(8,128)(2,1)}), bf16[8,2,48,96]{3,2,1,0:T(8,128)(2,1)S(1)}, u32[]{:S(2)}, u32[]{:S(2)}) async-start(bf16[8,2,48,96]{3,2,1,0:T(8,128)(2,1)} %copy.46), calls=%async_computation | async-start | bytes 393216 | tf_op jit(solution)/shard_map/all_to_all | solution.py:93
  148.7 21.4 %all-to-all-start.1 = ((bf16[8,2,48,384]{3,2,1,0:T(8,128)(2,1)}), bf16[8,2,48,384]{3,2,1,0:T(8,128)(2,1)S(1)}, u32[]{:S(2)}, u32[]{:S(2)}) async-start(bf16[8,2,48,384]{3,2,1,0:T(8,128)(2,1)} %copy.52), calls=%async_computation.2 | async-start | bytes 1179648 | tf_op jit(solution)/shard_map/all_to_all | solution.py:98
  153.3 56.0 %all-gather.3.cloned.1.call-start = ((), (), s32[]{:S(2)}) async-start(), calls=%async_computation.6 | async-start | bytes 1769472 | tf_op jit(solution)/shard_map/all_gather | solution.py:109
  174.2 11.7 %copy-start.2 = (s32[8]{0:T(128)S(1)}, s32[8]{0:T(128)}, u32[]{:S(2)}) copy-start(s32[8]{0:T(128)} %param.11) | copy-start | bytes 100
Sparse Core Ops, SparseCore 0:
  24.8 56.5 all-reduce.1
  112.6 33.8 reduce-scatter.1
  186.0 23.2 all-gather.2
where the time goes:
time: 242 us
  waiting for transfers between devices  126 us (52%)
  matrix products  56.8 us (23%)
  blocking collectives  24.8 us (10%)
  between operations  13.6 us (6%)
  starting transfers between devices  8.5 us (4%)
  local copies, waits for them, and re-layouts  8.36 us (3%)
  other arithmetic  3.9 us (2%)
    psum x1, waiting for transfers between devices, body(): bias = lax.psum(bias_part, ('chol', 'orb'))  56.4 us
    reduce_scatter x1, waiting for transfers between devices, body(): lax.psum_scatter(field_part, 'walk', scatter_dimension=0, tiled=True)  29.9 us
    dot_general x1, matrix products, body(): jnp.einsum('wcg,gab->wcab', coefficient, field_vectors, preferred_element...  29.4 us
    all_gather x1, waiting for transfers between devices, body(): lax.all_gather(summed.astype(jnp.bfloat16), ('chol', 'orb'), axis=2, tile...  23.3 us
    all_to_all x1, waiting for transfers between devices, body(): lax.all_to_all(spread, ('chol', 'orb'), split_axis=0, concat_axis=2, tile...  16.3 us
    all_to_all x1, blocking collectives, body(): lax.all_to_all(col_summed.astype(jnp.bfloat16), ('chol', 'orb'), split_ax...  10.7 us
    all_gather x1, blocking collectives, body(): all_theta = lax.all_gather(theta, 'walk', axis=0, tiled=True)  7.47 us
    dot_general x1, matrix products, body(): jnp.einsum('wcj,gj->wcg', all_theta, half_vectors, preferred_element_type...  7.2 us
  transfers between devices with their start and end apart: 5, of which 4 were waited for; matrix products, arithmetic and copies ran while one was open for 1% of the time, Pallas kernels for 0%

commit v1 on v0

--- a/solution.py
+++ b/solution.py
@@ -77,7 +77,7 @@
     bias_part = jnp.einsum(
         "wcj,gj->wcg", all_theta, half_vectors, preferred_element_type=jnp.float32
     )
-    bias = lax.psum(bias_part, ("chol", "orb"))
+    bias = jnp.sum(lax.all_gather(bias_part, ("chol", "orb")), axis=0)
     coefficient = jnp.stack([bias[:, 1], samples - bias[:, 0]], 1).astype(jnp.bfloat16)
     field_part = jnp.einsum(
         "wcg,gab->wcab", coefficient, field_vectors, preferred_element_type=jnp.float32

time: 242 us -> 210 us (0.87)
  waiting for transfers between devices: 126 us -> 93.7 us
    psum x1 -> x0, waiting for transfers between devices: 56.4 us -> none  [body(): bias = lax.psum(bias_part, ('chol', 'orb'))]
    all_gather x0 -> x1, waiting for transfers between devices: none -> 23.7 us  [body(): bias = jnp.sum(lax.all_gather(bias_part, ('chol', 'orb')), axis=0)]
  transfers between devices with their start and end apart: 5 -> 5, of which waited for: 4 -> 4; matrix products, arithmetic and copies ran while one was open for 1% -> 2% of each run, Pallas kernels for 0% -> 0%
where the time goes in v1:
time: 210 us; the launch traced here: 209 us
  waiting for transfers between devices  93.7 us (45%)
  matrix products  56.8 us (27%)
  blocking collectives  24.8 us (12%)
  between operations  13.6 us (6%)
  starting transfers between devices  8.48 us (4%)
  local copies, waits for them, and re-layouts  7.53 us (4%)
  other arithmetic  4.35 us (2%)
    reduce_scatter x1, waiting for transfers between devices, body(): lax.psum_scatter(field_part, 'walk', scatter_dimension=0, tiled=True)  30.4 us
    dot_general x1, matrix products, body(): jnp.einsum('wcg,gab->wcab', coefficient, field_vectors, preferred_element...  29.4 us
    all_gather x1, waiting for transfers between devices, body(): bias = jnp.sum(lax.all_gather(bias_part, ('chol', 'orb')), axis=0)  23.7 us
    all_gather x1, waiting for transfers between devices, body(): lax.all_gather(summed.astype(jnp.bfloat16), ('chol', 'orb'), axis=2, tile...  23.3 us
    all_to_all x1, waiting for transfers between devices, body(): lax.all_to_all(spread, ('chol', 'orb'), split_axis=0, concat_axis=2, tile...  16.3 us
    all_to_all x1, blocking collectives, body(): lax.all_to_all(col_summed.astype(jnp.bfloat16), ('chol', 'orb'), split_ax...  10.7 us
    all_gather x1, blocking collectives, body(): all_theta = lax.all_gather(theta, 'walk', axis=0, tiled=True)  7.47 us
    dot_general x1, matrix products, body(): jnp.einsum('wcj,gj->wcg', all_theta, half_vectors, preferred_element_type...  7.17 us
  transfers between devices with their start and end apart: 5, of which 4 were waited for; matrix products, arithmetic and copies ran while one was open for 2% of the time, Pallas kernels for 0%

profile of v1, /device:TPU:0, one launch (start us, length us, event | category | flops | bytes accessed | tf_op | source)
XLA Modules:
  0.0 209.2 jit_solution(9347680050240189926)
XLA Ops:
  6.5 1.1 copy.45
  7.8 0.5 fusion.37
  8.3 0.5 fusion.41
  8.7 0.5 fusion.29
  9.4 0.5 fusion.28
  10.0 7.5 %all_gather.15 = bf16[16,2,4608]{2,0,1:T(8,128)(2,1)S(1)} all-gather(bf16[8,2,4608]{2,0,1:T(8,128)(2,1)S(1)} %pad_maximum_fusion.1), channel_id=1, replica_groups=mesh['groups'=2,'chol'=4,'walk'=2,'orb'=2] {'walk'}, dimensions={0}, use_global_device_ids=true | all-gather | bytes 442368 | tf_op jit(solution)/shard_map/all_gather | solution.py:76
  17.5 7.2 %fusion.3 = f32[16,2,1024]{2,0,1:T(8,128)} fusion(bf16[16,2,4608]{2,0,1:T(8,128)(2,1)S(1)} %all_gather.15, bf16[1024,4608]{1,0:T(8,128)(2,1)} %param.8), kind=kOutput, calls=%fused_computation.4 | convolution fusion | flops 301989888 | bytes 9863168 | tf_op jit(solution)/shard_map/wcj,gj->wcg/dot_general | solution.py:77
  24.9 23.7 %all-gather.5.cloned.1.call-done = f32[128,2,1024]{2,0,1:T(8,128)} async-done(((f32[16,2,1024]{2,0,1:T(8,128)}), f32[128,2,1024]{2,0,1:T(8,128)}) %all-gather.5.cloned.1.call-update) | async-done | bytes 1048592 | tf_op jit(solution)/shard_map/all_gather | solution.py:80
  48.6 1.3 reduce_sum.19
  49.9 29.4 %fusion = f32[16,2,48,384]{3,0,2,1:T(8,128)} fusion(bf16[1024,48,384]{2,1,0:T(8,128)(2,1)} %param.9, bf16[16,1,1024]{2,0,1:T(8,128)(2,1)S(1)} %fusion.78, bf16[16,1,1024]{2,0,1:T(8,128)(2,1)S(1)} %slice.232), kind=kOutput, calls=%fused_computation.1 | convolution fusion | flops 1208090624 | bytes 40173568 | tf_op jit(solution)/shard_map/wcg,gab->wcab/dot_general | solution.py:82
  79.4 0.7 copy.46
  80.1 3.4 %all-to-all-start = ((bf16[8,2,48,96]{3,2,1,0:T(8,128)(2,1)}), bf16[8,2,48,96]{3,2,1,0:T(8,128)(2,1)S(1)}, u32[]{:S(2)}, u32[]{:S(2)}) async-start(bf16[8,2,48,96]{3,2,1,0:T(8,128)(2,1)} %copy.46), calls=%async_computation | async-start | bytes 393216 | tf_op jit(solution)/shard_map/all_to_all | solution.py:93
  83.5 30.4 %reduce-scatter.2.cloned.1.call-done = f32[8,2,48,384]{3,0,2,1:T(8,128)} async-done(((f32[16,2,48,384]{3,0,2,1:T(8,128)}), f32[8,2,48,384]{3,0,2,1:T(8,128)}) %reduce-scatter.2.cloned.1.call-update) | async-done | bytes 1179664 | tf_op jit(solution)/shard_map/reduce_scatter | solution.py:85
  113.9 1.3 convert_element_type.82
  115.2 0.9 copy.52
  116.1 4.6 %all-to-all-start.1 = ((bf16[8,2,48,384]{3,2,1,0:T(8,128)(2,1)}), bf16[8,2,48,384]{3,2,1,0:T(8,128)(2,1)S(1)}, u32[]{:S(2)}, u32[]{:S(2)}) async-start(bf16[8,2,48,384]{3,2,1,0:T(8,128)(2,1)} %copy.52), calls=%async_computation.2 | async-start | bytes 1179648 | tf_op jit(solution)/shard_map/all_to_all | solution.py:98
  120.7 0.3 all-gather.7.cloned.1.call-start
  121.2 16.3 %all-to-all-done.1 = bf16[8,2,48,384]{3,2,1,0:T(8,128)(2,1)S(1)} async-done(((bf16[8,2,48,384]{3,2,1,0:T(8,128)(2,1)}), bf16[8,2,48,384]{3,2,1,0:T(8,128)(2,1)S(1)}, u32[]{:S(2)}, u32[]{:S(2)}) %all-to-all-start.1) | async-done | bytes 589856 | tf_op jit(solution)/shard_map/all_to_all | solution.py:98
  137.5 0.3 fusion.65
  137.8 0.3 fusion.64
  138.1 0.3 fusion.26
  138.3 0.3 fusion.27
  138.9 0.2 fusion.72
  139.1 0.2 fusion.24
  139.3 0.2 fusion.25
  140.1 0.2 fusion.22
  140.3 0.2 fusion.23
  141.1 0.2 fusion.20
  141.8 10.7 %all_to_all.54 = bf16[1,2,384,96]{3,1,0,2:T(2,128)(2,1)S(1)} all-to-all(bf16[1,2,384,96]{3,1,0,2:T(2,128)(2,1)S(1)} %copy.54), channel_id=1, replica_groups=mesh['groups'=2,'chol'=4,'walk'=2,'orb'=2] {'chol','orb'}, dimensions={2} | all-to-all | bytes 294912 | tf_op jit(solution)/shard_map/all_to_all | solution.py:104
  152.6 0.7 copy.56
  153.4 23.3 %all-gather.7.cloned.1.call-done = bf16[8,1,2,384,96]{4,0,2,1,3:T(8,128)(2,1)} async-done(((bf16[8,1,2,48,96]{4,0,2,1,3:T(8,128)(2,1)}), bf16[8,1,2,384,96]{4,0,2,1,3:T(8,128)(2,1)}) %all-gather.7.cloned.1.call-update) | async-done | bytes 1179664 | tf_op jit(solution)/shard_map/all_gather | solution.py:109
  176.7 2.1 copy.57
  178.8 0.8 fusion.18
  179.6 0.8 fusion.16
  180.5 0.4 select_reduce_fusion
  180.9 0.4 fusion.7
  181.3 0.5 fusion.62
  181.8 0.5 fusion.58
  182.3 0.5 fusion.15
  182.8 0.5 fusion.60
  183.3 0.6 fusion.88
  183.9 0.5 fusion.52
  184.4 0.5 fusion.13
  184.9 0.6 fusion.87
  185.5 0.5 convolution_subtract_fusion.4
  186.0 0.5 convolution_subtract_fusion.3
  186.5 0.5 convolution_add_fusion.4
  187.0 0.5 convolution_add_fusion.3
  187.5 0.5 fusion.89
  188.1 0.5 fusion.91
  188.6 0.5 fusion.12
  189.1 0.5 fusion.92
  189.7 0.5 fusion.90
  190.2 0.5 fusion.10
  190.8 0.5 fusion.8
  191.3 0.8 fusion.9
  192.1 0.3 fusion.66
  192.5 0.3 fusion.67
  192.8 0.3 fusion.31
  193.2 0.3 fusion.30
  193.7 0.3 pad_maximum_fusion.2
  194.1 6.6 %all_gather.19 = bf16[16,2,4608]{2,1,0:T(2,128)(2,1)S(1)} all-gather(bf16[8,2,4608]{2,1,0:T(2,128)(2,1)S(1)} %pad_maximum_fusion.2), channel_id=1, replica_groups=mesh['groups'=2,'chol'=4,'walk'=2,'orb'=2] {'walk'}, dimensions={0}, use_global_device_ids=true | all-gather | bytes 442368 | tf_op jit(solution)/shard_map/all_gather | solution.py:124
  200.9 0.9 gather_fusion
  201.8 0.9 broadcast_select_fusion
  (44 shorter events, 3.4 us)
Async XLA Ops:
  6.5 1.3 copy-start
  6.5 42.1 %all-gather.5.cloned.1.call-start = ((), (), s32[]{:S(2)}) async-start(), calls=%async_computation.5 | async-start | bytes 1179648 | tf_op jit(solution)/shard_map/all_gather | solution.py:80
  24.7 25.2 %copy-start.1 = (f32[16,1024]{1,0:T(8,128)S(1)}, f32[16,1024]{1,0:T(8,128)}, u32[]{:S(2)}) copy-start(f32[16,1024]{1,0:T(8,128)} %param.10) | copy-start | bytes 196612
  24.7 89.2 %reduce-scatter.2.cloned.1.call-start = ((), (), s32[]{:S(2)}) async-start(), calls=%async_computation.4 | async-start | bytes 3538944 | tf_op jit(solution)/shard_map/reduce_scatter | solution.py:85
  80.1 36.0 %all-to-all-start = ((bf16[8,2,48,96]{3,2,1,0:T(8,128)(2,1)}), bf16[8,2,48,96]{3,2,1,0:T(8,128)(2,1)S(1)}, u32[]{:S(2)}, u32[]{:S(2)}) async-start(bf16[8,2,48,96]{3,2,1,0:T(8,128)(2,1)} %copy.46), calls=%async_computation | async-start | bytes 393216 | tf_op jit(solution)/shard_map/all_to_all | solution.py:93
  116.1 21.3 %all-to-all-start.1 = ((bf16[8,2,48,384]{3,2,1,0:T(8,128)(2,1)}), bf16[8,2,48,384]{3,2,1,0:T(8,128)(2,1)S(1)}, u32[]{:S(2)}, u32[]{:S(2)}) async-start(bf16[8,2,48,384]{3,2,1,0:T(8,128)(2,1)} %copy.52), calls=%async_computation.2 | async-start | bytes 1179648 | tf_op jit(solution)/shard_map/all_to_all | solution.py:98
  120.7 56.0 %all-gather.7.cloned.1.call-start = ((), (), s32[]{:S(2)}) async-start(), calls=%async_computation.6 | async-start | bytes 1769472 | tf_op jit(solution)/shard_map/all_gather | solution.py:109
  141.6 11.7 %copy-start.2 = (s32[8]{0:T(128)S(1)}, s32[8]{0:T(128)}, u32[]{:S(2)}) copy-start(s32[8]{0:T(128)} %param.11) | copy-start | bytes 100
Sparse Core Ops, SparseCore 0:
  24.8 23.7 all-gather.4
  79.5 34.3 reduce-scatter.1
  153.4 23.2 all-gather.6
